TPU v7x, 512 devices: a whole 4x4x16 slice. The times are simulated.
512 devices in a mesh: pts: 16 (over x, z_hi, core), ctr: 32 (over z_lo, y).
Axes of the slice: x: 4, y: 4, z: 16 (z_hi: 2, z_lo: 8; z = z_hi * 8 + z_lo), core: 2. Of those that a mesh axis runs over, the one named last changes fastest.
Arguments:
- points: float32 [8192, 256], P('pts'), may hold values from -6 to 6
- labels: bfloat16 [8192, 256], P('pts'), may hold values from -6 to 6
- centres: float32 [2, 4096, 256], P(None, 'ctr'), may hold values from -6 to 6
- coeffs: float32 [2, 4096, 256], P(None, 'pts'), may hold values from -6 to 6
- diag_inverse: float32 [2, 4096, 4096], P(None, 'ctr', 'pts'), may hold values from -0.09375 to 0.09375
- off_block: float32 [4096, 4096], P('pts', 'ctr'), may hold values from -0.09375 to 0.09375
Outputs:
- transposed: float32 [2, 4096, 256], P(None, 'ctr', 'pts')
All inputs are finite; a program needn't handle non-finite values.
Results may differ from a plain program's by a relative error of at most 0.0003.
Values sent between devices are 32-bit elements; how exact they have to be, the bound alone decides.
No kernel may reach another device: no remote copies, remote signals or barrier semaphores. Data moves between devices by JAX's collectives and lax.ppermute only.
A program may use at most 64 MiB of HBM per device.

v0:
```python
import math
import jax
import jax.numpy as jnp
from jax import lax
from jax.sharding import PartitionSpec as P


def kernel_tile(points, flat_centres):
    score = lax.dot_general(
        points,
        flat_centres,
        (((1,), (1,)), ((), ())),
        precision=lax.Precision.HIGHEST,
        preferred_element_type=jnp.float32,
    ) / math.sqrt(points.shape[1])
    return score + score * score * score / 3.0


def local(points, labels, centres, coeffs, diag_inverse, off_block):
    high = lax.Precision.HIGHEST
    panels = centres.shape[0]
    local_rows = centres.shape[1]
    flat_centres = centres.reshape(panels * local_rows, centres.shape[2])
    kernel = kernel_tile(points, flat_centres)
    second = lax.psum(
        jnp.dot(diag_inverse[1], coeffs[1], precision=high, preferred_element_type=jnp.float32),
        "pts",
    )
    carried = lax.psum(
        jnp.dot(off_block, second, precision=high, preferred_element_type=jnp.float32), "ctr"
    )
    rest = coeffs[0] - carried
    first = lax.psum(
        jnp.dot(diag_inverse[0], rest, precision=high, preferred_element_type=jnp.float32), "pts"
    )
    solved = jnp.concatenate([first, second], axis=0)
    total_centres = panels * local_rows * lax.axis_size("ctr")
    pred_scale = 1.0 / (2.0 * math.sqrt(total_centres))
    partial_pred = jnp.dot(kernel, solved, precision=high, preferred_element_type=jnp.float32)
    pred = lax.psum(partial_pred, "ctr")
    weights = jnp.tanh(pred * pred_scale - labels.astype(jnp.float32))
    total_points = points.shape[0] * lax.axis_size("pts")
    term = lax.dot_general(
        kernel,
        weights,
        (((0,), (0,)), ((), ())),
        precision=high,
        preferred_element_type=jnp.float32,
    )
    term = term.reshape(panels, local_rows, weights.shape[1])
    summed = lax.psum_scatter(term, "pts", scatter_dimension=2, tiled=True)
    return summed / (2.0 * math.sqrt(total_points))


def solution(mesh):
    return jax.shard_map(
        local,
        mesh=mesh,
        in_specs=(
            P("pts", None),
            P("pts", None),
            P(None, "ctr", None),
            P(None, "pts", None),
            P(None, "ctr", "pts"),
            P("pts", "ctr"),
        ),
        out_specs=P(None, "ctr", "pts"),
        check_vma=False,
    )
```

profile of v0, /device:TPU:8, one launch (start us, length us, event | category | flops | bytes accessed | tf_op | source)
XLA Modules:
  0.0 1540.9 jit_solution(7603430247279964926)
XLA Ops:
  6.5 0.0 copy-start
  6.5 0.0 all-reduce.5.cloned.1.call-start
  6.5 0.0 copy-start.6
  6.5 2.0 fusion.11
  8.6 0.0 copy-start.1
  8.6 0.0 all-reduce.5.cloned.1.call-update
  8.6 0.0 all-reduce.7.cloned.1.call-start
  8.6 259.4 %all-reduce.5.cloned.1.call-done = f32[128,256]{1,0:T(8,128)} async-done(((f32[128,256]{1,0:T(8,128)}), f32[128,256]{1,0:T(8,128)}) %all-reduce.5.cloned.1.call-update) | async-done | bytes 131088 | tf_op jit(solution)/shard_map/psum | solution.py:25
  268.0 0.0 copy-done.6
  268.0 2.0 convolution_bitcast_fusion
  270.0 0.0 copy-start.4
  270.0 0.0 all-reduce.7.cloned.1.call-update
  270.0 0.0 all-reduce.9.cloned.1.call-start
  270.1 452.3 %all-reduce.7.cloned.1.call-done = f32[256,256]{1,0:T(8,128)} async-done(((f32[256,256]{1,0:T(8,128)}), f32[256,256]{1,0:T(8,128)}) %all-reduce.7.cloned.1.call-update) | async-done | bytes 262160 | tf_op jit(solution)/shard_map/psum | solution.py:29
  722.4 0.0 copy-done.1
  722.4 0.0 copy-done.4
  722.4 0.0 copy-start.3
  722.4 2.0 convolution_bitcast_fusion.1
  724.4 0.0 all-reduce.9.cloned.1.call-update
  724.4 0.0 all-reduce.11.cloned.1.call-start
  724.5 0.0 copy-done
  724.5 0.0 copy-done.3
  724.5 0.0 copy-start.2
  724.5 0.6 fusion.1
  725.1 251.9 %all-reduce.9.cloned.1.call-done = f32[128,256]{1,0:T(8,128)} async-done(((f32[128,256]{1,0:T(8,128)}), f32[128,256]{1,0:T(8,128)}) %all-reduce.9.cloned.1.call-update) | async-done | bytes 131088 | tf_op jit(solution)/shard_map/psum | solution.py:33
  977.1 0.0 copy-done.2
  977.1 2.3 fusion.7
  979.4 0.0 copy-start.5
  979.4 0.0 all-reduce.11.cloned.1.call-update
  979.4 0.0 reduce-scatter.2.cloned.1.call-start
  979.4 453.7 %all-reduce.11.cloned.1.call-done = f32[512,256]{1,0:T(8,128)} async-done(((f32[512,256]{1,0:T(8,128)}), f32[512,256]{1,0:T(8,128)}) %all-reduce.11.cloned.1.call-update) | async-done | bytes 524304 | tf_op jit(solution)/shard_map/psum | solution.py:40
  1433.2 0.0 copy-done.5
  1433.2 2.0 fusion.2
  1435.2 0.8 copy.7
  1436.0 0.0 reduce-scatter.2.cloned.1.call-update
  1436.1 96.9 %reduce-scatter.2.cloned.1.call-done = f32[2,128,16]{1,2,0:T(8,128)} async-done(((f32[2,128,256]{1,2,0:T(8,128)}), f32[2,128,16]{1,2,0:T(8,128)}) %reduce-scatter.2.cloned.1.call-update) | async-done | bytes 16400 | tf_op jit(solution)/shard_map/reduce_scatter | solution.py:51
  1533.0 1.3 broadcast_multiply_fusion
Async XLA Ops:
  6.5 717.9 %copy-start = (f32[512,256]{1,0:T(8,128)S(1)}, f32[512,256]{1,0:T(8,128)}, u32[]{:S(2)}) copy-start(f32[512,256]{1,0:T(8,128)} %param.6) | copy-start | bytes 1572868
  6.5 261.5 %all-reduce.5.cloned.1.call-start = ((), (), s32[]{:S(2)}) async-start(), calls=%async_computation.1 | async-start | bytes 262144 | tf_op jit(solution)/shard_map/psum | solution.py:25
  6.5 261.5 %copy-start.6 = (f32[256,128]{1,0:T(8,128)S(1)}, f32[256,128]{1,0:T(8,128)}, u32[]{:S(2)}) copy-start(f32[256,128]{1,0:T(8,128)} %param.11) | copy-start | bytes 393220
  8.6 713.9 %copy-start.1 = (f32[2,256,256]{2,1,0:T(8,128)S(1)}, f32[2,256,256]{2,1,0:T(8,128)}, u32[]{:S(2)}) copy-start(f32[2,256,256]{2,1,0:T(8,128)} %param.9) | copy-start | bytes 1572868
  8.6 713.8 %all-reduce.7.cloned.1.call-start = ((), (), s32[]{:S(2)}) async-start(), calls=%async_computation.2 | async-start | bytes 524288 | tf_op jit(solution)/shard_map/psum | solution.py:29
  270.0 452.4 %copy-start.4 = (f32[2,128,256]{2,1,0:T(8,128)S(1)}, f32[2,128,256]{2,1,0:T(8,128)}, u32[]{:S(2)}) copy-start(f32[2,128,256]{2,1,0:T(8,128)} %param.10) | copy-start | bytes 786436
  270.0 707.0 %all-reduce.9.cloned.1.call-start = ((), (), s32[]{:S(2)}) async-start(), calls=%async_computation.3 | async-start | bytes 262144 | tf_op jit(solution)/shard_map/psum | solution.py:33
  722.4 2.0 copy-start.3
  724.4 708.7 %all-reduce.11.cloned.1.call-start = ((), (), s32[]{:S(2)}) async-start(), calls=%async_computation.4 | async-start | bytes 1048576 | tf_op jit(solution)/shard_map/psum | solution.py:40
  724.5 252.6 %copy-start.2 = (f32[128,256]{1,0:T(8,128)S(1)}, f32[128,256]{1,0:T(8,128)}, u32[]{:S(2)}) copy-start(f32[128,256]{1,0:T(8,128)} %all-reduce.5.cloned.1.call-done) | copy-start | bytes 393220
  979.4 453.8 %copy-start.5 = (bf16[512,256]{1,0:T(8,128)(2,1)S(1)}, bf16[512,256]{1,0:T(8,128)(2,1)}, u32[]{:S(2)}) copy-start(bf16[512,256]{1,0:T(8,128)(2,1)} %param.7) | copy-start | bytes 786436
  979.4 553.6 %reduce-scatter.2.cloned.1.call-start = ((), (), s32[]{:S(2)}) async-start(), calls=%async_computation.5 | async-start | bytes 278528 | tf_op jit(solution)/shard_map/reduce_scatter | solution.py:51
Sparse Core Ops, SparseCore 0:
  10.3 257.7 all-reduce.4
  271.2 451.2 all-reduce.6
  725.3 251.7 all-reduce.8
  980.1 453.0 all-reduce.10
  1437.6 95.3 reduce-scatter.1
where the time goes:
time: 1540 us
  waiting for transfers between devices  1510 us (98%)
    psum x1, waiting for transfers between devices, local(): pred = lax.psum(partial_pred, 'ctr')  454 us
    psum x1, waiting for transfers between devices, local(): lax.psum(jnp.dot(off_block, second, precision=high, preferred_element_typ...  452 us
    psum x1, waiting for transfers between devices, local(): lax.psum(jnp.dot(diag_inverse[1], coeffs[1], precision=high, preferred_el...  259 us
    psum x1, waiting for transfers between devices, local(): lax.psum(jnp.dot(diag_inverse[0], rest, precision=high, preferred_element...  252 us
    reduce_scatter x1, waiting for transfers between devices, local(): summed = lax.psum_scatter(term, 'pts', scatter_dimension=2, tiled=True)  96.9 us
  transfers between devices with their start and end apart: 5, of which 5 were waited for; matrix products, arithmetic and copies ran while one was open for 0% of the time, Pallas kernels for 0%

commit v1 on v0

--- a/solution.py
+++ b/solution.py
@@ -37,7 +37,8 @@
     total_centres = panels * local_rows * lax.axis_size("ctr")
     pred_scale = 1.0 / (2.0 * math.sqrt(total_centres))
     partial_pred = jnp.dot(kernel, solved, precision=high, preferred_element_type=jnp.float32)
-    pred = lax.psum(partial_pred, "ctr")
+    review_plane = lambda chunk: jnp.sum(lax.all_gather(chunk, "ctr"), 0)
+    pred = review_plane(partial_pred)
     weights = jnp.tanh(pred * pred_scale - labels.astype(jnp.float32))
     total_points = points.shape[0] * lax.axis_size("pts")
     term = lax.dot_general(

time: 1540 us -> 1340 us (0.87)
  waiting for transfers between devices: 1510 us -> 1310 us
    psum x1 -> x0, waiting for transfers between devices: 454 us -> none  [local(): pred = lax.psum(partial_pred, 'ctr')]
    all_gather x0 -> x1, waiting for transfers between devices: none -> 254 us  [local(): review_plane = lambda chunk: jnp.sum(lax.all_gather(chunk, 'ctr'), 0)]
where the time goes in v1:
time: 1340 us
  waiting for transfers between devices  1310 us (98%)
    psum x1, waiting for transfers between devices, local(): lax.psum(jnp.dot(off_block, second, precision=high, preferred_element_typ...  452 us
    psum x1, waiting for transfers between devices, local(): lax.psum(jnp.dot(diag_inverse[1], coeffs[1], precision=high, preferred_el...  259 us
    all_gather x1, waiting for transfers between devices, local(): review_plane = lambda chunk: jnp.sum(lax.all_gather(chunk, 'ctr'), 0)  254 us
    psum x1, waiting for transfers between devices, local(): lax.psum(jnp.dot(diag_inverse[0], rest, precision=high, preferred_element...  251 us
    reduce_scatter x1, waiting for transfers between devices, local(): summed = lax.psum_scatter(term, 'pts', scatter_dimension=2, tiled=True)  94.3 us
  transfers between devices with their start and end apart: 5, of which 5 were waited for; matrix products, arithmetic and copies ran while one was open for 0% of the time, Pallas kernels for 0%

profile of v1, /device:TPU:8, one launch (start us, length us, event | category | flops | bytes accessed | tf_op | source)
XLA Modules:
  0.0 1344.6 jit_solution(15388619705694062944)
XLA Ops:
  6.5 0.0 copy-start
  6.5 0.0 copy-start.1
  6.5 0.0 all-reduce.4.cloned.1.call-start
  6.5 2.0 fusion.11
  8.6 0.0 all-reduce.4.cloned.1.call-update
  8.6 0.0 all-reduce.6.cloned.1.call-start
  8.6 259.4 %all-reduce.4.cloned.1.call-done = f32[128,256]{1,0:T(8,128)} async-done(((f32[128,256]{1,0:T(8,128)}), f32[128,256]{1,0:T(8,128)}) %all-reduce.4.cloned.1.call-update) | async-done | bytes 131088 | tf_op jit(solution)/shard_map/psum | solution.py:25
  268.0 2.0 convolution_bitcast_fusion
  270.1 0.0 all-reduce.6.cloned.1.call-update
  270.1 0.0 all-reduce.8.cloned.1.call-start
  270.1 452.3 %all-reduce.6.cloned.1.call-done = f32[256,256]{1,0:T(8,128)} async-done(((f32[256,256]{1,0:T(8,128)}), f32[256,256]{1,0:T(8,128)}) %all-reduce.6.cloned.1.call-update) | async-done | bytes 262160 | tf_op jit(solution)/shard_map/psum | solution.py:29
  722.4 2.0 convolution_bitcast_fusion.1
  724.5 0.0 all-reduce.8.cloned.1.call-update
  724.5 0.0 all-gather.3.cloned.1.call-start
  724.5 0.0 copy-done
  724.6 1.6 fusion.1
  726.2 250.9 %all-reduce.8.cloned.1.call-done = f32[128,256]{1,0:T(8,128)} async-done(((f32[128,256]{1,0:T(8,128)}), f32[128,256]{1,0:T(8,128)}) %all-reduce.8.cloned.1.call-update) | async-done | bytes 131088 | tf_op jit(solution)/shard_map/psum | solution.py:33
  977.1 2.3 fusion.7
  979.4 0.0 all-gather.3.cloned.1.call-update
  979.4 0.0 reduce-scatter.2.cloned.1.call-start
  979.5 254.3 %all-gather.3.cloned.1.call-done = f32[16384,256]{1,0:T(8,128)} async-done(((f32[512,256]{1,0:T(8,128)}), f32[16384,256]{1,0:T(8,128)}) %all-gather.3.cloned.1.call-update) | async-done | bytes 16777232 | tf_op jit(solution)/shard_map/all_gather | solution.py:40
  1233.7 6.9 reduce_sum.9
  1240.6 0.0 copy-done.1
  1240.7 1.0 fusion.2
  1241.7 0.8 copy.7
  1242.5 0.0 reduce-scatter.2.cloned.1.call-update
  1242.5 94.3 %reduce-scatter.2.cloned.1.call-done = f32[2,128,16]{1,2,0:T(8,128)} async-done(((f32[2,128,256]{1,2,0:T(8,128)}), f32[2,128,16]{1,2,0:T(8,128)}) %reduce-scatter.2.cloned.1.call-update) | async-done | bytes 16400 | tf_op jit(solution)/shard_map/reduce_scatter | solution.py:52
  1336.8 1.3 broadcast_multiply_fusion
Async XLA Ops:
  6.5 718.0 %copy-start = (f32[512,256]{1,0:T(8,128)S(1)}, f32[512,256]{1,0:T(8,128)}, u32[]{:S(2)}) copy-start(f32[512,256]{1,0:T(8,128)} %param.6) | copy-start | bytes 1572868
  6.5 1234.1 %copy-start.1 = (bf16[512,256]{1,0:T(8,128)(2,1)S(1)}, bf16[512,256]{1,0:T(8,128)(2,1)}, u32[]{:S(2)}) copy-start(bf16[512,256]{1,0:T(8,128)(2,1)} %param.7) | copy-start | bytes 786436
  6.5 261.5 %all-reduce.4.cloned.1.call-start = ((), (), s32[]{:S(2)}) async-start(), calls=%async_computation.1 | async-start | bytes 262144 | tf_op jit(solution)/shard_map/psum | solution.py:25
  8.6 713.8 %all-reduce.6.cloned.1.call-start = ((), (), s32[]{:S(2)}) async-start(), calls=%async_computation.2 | async-start | bytes 524288 | tf_op jit(solution)/shard_map/psum | solution.py:29
  270.1 707.0 %all-reduce.8.cloned.1.call-start = ((), (), s32[]{:S(2)}) async-start(), calls=%async_computation.3 | async-start | bytes 262144 | tf_op jit(solution)/shard_map/psum | solution.py:33
  724.5 509.3 %all-gather.3.cloned.1.call-start = ((), (), s32[]{:S(2)}) async-start(), calls=%async_computation.5 | async-start | bytes 17301504 | tf_op jit(solution)/shard_map/all_gather | solution.py:40
  979.4 357.3 %reduce-scatter.2.cloned.1.call-start = ((), (), s32[]{:S(2)}) async-start(), calls=%async_computation.4 | async-start | bytes 278528 | tf_op jit(solution)/shard_map/reduce_scatter | solution.py:52
Sparse Core Ops, SparseCore 0:
  10.3 257.7 all-reduce.3
  271.2 451.2 all-reduce.5
  725.3 251.7 all-reduce.7
  979.6 254.1 all-gather.2
  1242.6 94.1 reduce-scatter.1
